TPU v7x, 32 devices: a whole 2x2x4 slice. The times are simulated.
32 devices in a mesh: seq: 16 (over z, y, x), dp: 2 (over core).
Axes of the slice: x: 2, y: 2, z: 4, core: 2. Of those that a mesh axis runs over, the one named last changes fastest.
Arguments:
- inputs: bfloat16 [8, 1536, 896], P('dp', 'seq'), may hold values from -6 to 6
- lengths: int32 [8, 9], P('dp'), may hold values from 0 to 1536, as said below
- w_qkv: bfloat16 [896, 1152], replicated, may hold values from -0.1875 to 0.1875
- b_qkv: bfloat16 [1152], replicated, may hold values from -3 to 3
- g_attn: bfloat16 [896], replicated, may hold values from 0.25 to 1.75
- w_out: bfloat16 [896, 896], replicated, may hold values from -1.5 to 1.5
- g_mlp: bfloat16 [896], replicated, may hold values from 0.25 to 1.75
- w_gate_up: bfloat16 [896, 9728], replicated, may hold values from -0.1875 to 0.1875
- w_down: bfloat16 [4864, 896], replicated, may hold values from -0.078125 to 0.078125
- cotangent: bfloat16 [8, 1536, 896], P('dp', 'seq'), may hold values from -6 to 6
Outputs:
- output: bfloat16 [8, 1536, 896], P('dp', 'seq')
- grad_input: float32 [8, 1536, 896], P('dp', 'seq')
- grad_qkv: float32 [896, 1152], P('seq')
- grad_bias_qkv: float32 [1152], replicated
- grad_norm_attn: float32 [896], replicated
- grad_out: float32 [896, 896], P('seq')
- grad_norm_mlp: float32 [896], replicated
- grad_gate_up: float32 [896, 9728], P('seq')
- grad_down: float32 [4864, 896], P('seq')
Inputs may be any that keep to these rules, and one draw needn't show every extreme that they name: Each row lists the lengths of the documents packed one after another from the start of a stream; nonzero entries come first, and the tokens after their sum, fewer than 96, are padding. In every group of 4 consecutive rows one row is a single document of 1536 tokens; any other document has at most 4096 tokens.
All inputs are finite; a program needn't handle non-finite values.
Results may differ from a plain program's by a relative error of at most 0.014.
Values may be sent and summed in bfloat16 or wider, within the bound.
No kernel may reach another device: no remote copies, remote signals or barrier semaphores. Data moves between devices by JAX's collectives and lax.ppermute only.
A program may use at most 576 MiB of HBM per device.

v0:
```python
import jax
import jax.numpy as jnp
from jax import lax
from jax.sharding import PartitionSpec as P

HEADS = 14
KVH = 2
HD = 64
FF = 4864
epsilon = 1e-06
rope_base = 1000000.0


def cut_along(shard, dim, devices):
    before, after = (shard.shape[:dim], shard.shape[dim + 1 :])
    return jnp.moveaxis(shard.reshape(*before, devices, -1, *after), dim, 0)


def summed_on_arrival(shard, axis, dim):
    devices = lax.axis_size(axis)
    blocks = lax.all_to_all(cut_along(shard, dim, devices), axis, 0, 0, tiled=True)
    return jnp.sum(blocks.astype(jnp.float32), axis=0)


def layout(lengths, offset, row_count):
    places = offset + jnp.arange(row_count, dtype=jnp.int32)
    ends = jnp.cumsum(lengths, axis=-1, dtype=jnp.int32)
    after = (places[None, :, None] >= ends[:, None, :]).astype(jnp.int32)
    segment = jnp.sum(after, axis=-1, dtype=jnp.int32)
    begins = jnp.sum(after * lengths[:, None, :], axis=-1, dtype=jnp.int32)
    return (segment, places[None, :] - begins, places[None, :] < ends[:, -1:])


def tables(position, head_size):
    half = head_size // 2
    inverse = rope_base ** (-(jnp.arange(half, dtype=jnp.float32) * (2.0 / head_size)))
    angle = position.astype(jnp.float32)[..., None] * inverse
    return (jnp.cos(angle)[..., None, :], jnp.sin(angle)[..., None, :])


def rotate(field, cos_table, sin_table):
    half = field.shape[-1] // 2
    first = field[..., :half]
    second = field[..., half:]
    return jnp.concatenate(
        [first * cos_table - second * sin_table, second * cos_table + first * sin_table], axis=-1
    )


def unrotate(grad_field, cos_table, sin_table):
    half = grad_field.shape[-1] // 2
    first = grad_field[..., :half]
    second = grad_field[..., half:]
    return jnp.concatenate(
        [first * cos_table + second * sin_table, second * cos_table - first * sin_table], axis=-1
    )


def transposed_product(left, right):
    return lax.dot_general(
        left, right, (((1,), (1,)), ((), ())), preferred_element_type=jnp.float32
    )


def shards(inputs, lengths, w_qkv, b_qkv, g_attn, w_out, g_mlp, w_gate_up, w_down, cotangent):
    streams, length, model_width = inputs.shape
    tokens = streams * length
    stream_len = length * lax.axis_size("seq")
    offset = lax.axis_index("seq") * length
    q_width = HEADS * HD
    kv_width = KVH * HD
    group_size = HEADS // KVH
    factor = HD ** (-0.5)
    blocks = max(1, min(16, stream_len // 512))
    key_block = stream_len // blocks
    q_seg, q_pos, valid_rows = layout(lengths, offset, length)
    k_seg, unused_pos, unused_valid = layout(lengths, 0, stream_len)
    q_place = offset + jnp.arange(length, dtype=jnp.int32)
    residual = inputs.reshape(tokens, model_width).astype(jnp.float32)
    inv_attn = lax.rsqrt(jnp.mean(residual * residual, axis=-1, keepdims=True) + epsilon)
    unit_attn = residual * inv_attn
    gain_attn = g_attn.astype(jnp.float32)
    normed = (unit_attn * gain_attn).astype(jnp.bfloat16)
    projected = jnp.dot(normed, w_qkv, preferred_element_type=jnp.float32) + b_qkv.astype(
        jnp.float32
    )
    cos_table, sin_table = tables(q_pos.reshape(tokens), HD)
    q_rot = rotate(projected[:, :q_width].reshape(tokens, HEADS, HD), cos_table, sin_table)
    k_rot = rotate(
        projected[:, q_width : q_width + kv_width].reshape(tokens, KVH, HD), cos_table, sin_table
    )
    queries = q_rot.astype(jnp.bfloat16).reshape(streams, length, KVH, group_size, HD)
    key_low = k_rot.astype(jnp.bfloat16).reshape(streams, length, kv_width)
    value_low = (
        projected[:, q_width + kv_width :].astype(jnp.bfloat16).reshape(streams, length, kv_width)
    )
    key_all, value_all = (
        lax.all_gather(key_low, "seq", axis=1, tiled=True),
        lax.all_gather(value_low, "seq", axis=1, tiled=True),
    )
    key_all = key_all.reshape(streams, stream_len, KVH, HD)
    value_all = value_all.reshape(streams, stream_len, KVH, HD)

    def scored(key_part, key_seg, first_key, rows):
        scores = (
            jnp.einsum("bqhgd,bkhd->bhgqk", queries, key_part, preferred_element_type=jnp.float32)
            * factor
        )
        key_place = first_key + jnp.arange(rows, dtype=jnp.int32)
        allowed = (q_seg[:, :, None] == key_seg[:, None, :]) & (
            q_place[None, :, None] >= key_place[None, None, :]
        )
        return (scores, allowed[:, None, None])

    def touches(first_key, rows):
        last_seg = lax.dynamic_slice_in_dim(k_seg, first_key + rows - 1, 1, 1)[:, 0]
        return jnp.any((first_key <= q_place[length - 1]) & (last_seg >= q_seg[:, 0]))

    def slices(first_key, rows, key_src, value_src):
        return (
            lax.dynamic_slice_in_dim(key_src, first_key, rows, 1),
            lax.dynamic_slice_in_dim(value_src, first_key, rows, 1),
            lax.dynamic_slice_in_dim(k_seg, first_key, rows, 1),
        )

    def softmax_stats(block_index, running):
        first_key = block_index * key_block

        def softmax_compute(state):
            row_max, row_sum = state
            key_part, unused_value, key_seg = slices(first_key, key_block, key_all, value_all)
            scores, allowed = scored(key_part, key_seg, first_key, key_block)
            masked = jnp.where(allowed, scores, -1e30)
            new_max = jnp.maximum(row_max, jnp.max(masked, axis=-1, keepdims=True))
            fresh = jnp.where(allowed, jnp.exp(masked - new_max), 0.0)
            return (
                new_max,
                row_sum * jnp.exp(row_max - new_max) + jnp.sum(fresh, axis=-1, keepdims=True),
            )

        return lax.cond(
            touches(first_key, key_block), softmax_compute, lambda state: state, running
        )

    stat_shape = (streams, KVH, group_size, length, 1)
    row_max, row_sum = lax.fori_loop(
        0,
        blocks,
        softmax_stats,
        (jnp.full(stat_shape, -1e30, jnp.float32), jnp.zeros(stat_shape, jnp.float32)),
    )
    log_sum = row_max + jnp.log(row_sum)

    def weighted(block_index, running):
        first_key = block_index * key_block

        def weighted_compute(partial_value):
            key_part, value_part, key_seg = slices(first_key, key_block, key_all, value_all)
            scores, allowed = scored(key_part, key_seg, first_key, key_block)
            weights = jnp.where(allowed, jnp.exp(scores - log_sum), 0.0).astype(jnp.bfloat16)
            return partial_value + jnp.einsum(
                "bhgqk,bkhd->bqhgd", weights, value_part, preferred_element_type=jnp.float32
            )

        return lax.cond(
            touches(first_key, key_block),
            weighted_compute,
            lambda partial_value: partial_value,
            running,
        )

    mixed_out = lax.fori_loop(
        0, blocks, weighted, jnp.zeros((streams, length, KVH, group_size, HD), jnp.float32)
    )
    mixed_low = mixed_out.reshape(tokens, q_width).astype(jnp.bfloat16)
    middle = residual + jnp.dot(mixed_low, w_out, preferred_element_type=jnp.float32)
    inv_mlp = lax.rsqrt(jnp.mean(middle * middle, axis=-1, keepdims=True) + epsilon)
    unit_mlp = middle * inv_mlp
    gain_mlp = g_mlp.astype(jnp.float32)
    normed_mlp = (unit_mlp * gain_mlp).astype(jnp.bfloat16)
    gate_up = jnp.dot(normed_mlp, w_gate_up, preferred_element_type=jnp.float32)
    gate_pre = gate_up[:, :FF]
    up_pre = gate_up[:, FF:]
    gate_sigmoid = jax.nn.sigmoid(gate_pre)
    gate_silu = jax.nn.silu(gate_pre)
    active = (gate_silu * up_pre).astype(jnp.bfloat16)
    output = (middle + jnp.dot(active, w_down, preferred_element_type=jnp.float32)).astype(
        jnp.bfloat16
    )
    seed_grad = (cotangent * valid_rows[..., None].astype(jnp.bfloat16)).reshape(
        tokens, model_width
    )
    grad_active = transposed_product(seed_grad, w_down)
    grad_gate = grad_active * up_pre * (gate_sigmoid * (1.0 + gate_pre * (1.0 - gate_sigmoid)))
    grad_up = grad_active * gate_silu
    grad_gate_up = jnp.concatenate([grad_gate, grad_up], axis=1).astype(jnp.bfloat16)
    grad_normed_mlp = transposed_product(grad_gate_up, w_gate_up)
    scaled_mlp = grad_normed_mlp * gain_mlp
    grad_middle = seed_grad.astype(jnp.float32) + inv_mlp * (
        scaled_mlp - unit_mlp * jnp.mean(scaled_mlp * unit_mlp, axis=-1, keepdims=True)
    )
    gain_mlp_part = jnp.sum(grad_normed_mlp * unit_mlp, axis=0)
    grad_branch = grad_middle.astype(jnp.bfloat16)
    grad_mixed = (
        transposed_product(grad_branch, w_out)
        .astype(jnp.bfloat16)
        .reshape(streams, length, KVH, group_size, HD)
    )
    row_delta = jnp.sum(grad_mixed.astype(jnp.float32) * mixed_out, axis=-1).transpose(0, 2, 3, 1)[
        ..., None
    ]
    key_back, value_back = (
        lax.all_gather(key_low, "seq", axis=1, tiled=True),
        lax.all_gather(value_low, "seq", axis=1, tiled=True),
    )
    key_back = key_back.reshape(streams, stream_len, KVH, HD)
    value_back = value_back.reshape(streams, stream_len, KVH, HD)

    def back_block(block_index, running):
        first_key = block_index * key_block

        def back_compute(state):
            query_grads, key_terms_all = state
            key_part, value_part, key_seg = slices(first_key, key_block, key_back, value_back)
            scores, allowed = scored(key_part, key_seg, first_key, key_block)
            weights = jnp.where(allowed, jnp.exp(scores - log_sum), 0.0)
            grad_weights = jnp.einsum(
                "bqhgd,bkhd->bhgqk", grad_mixed, value_part, preferred_element_type=jnp.float32
            )
            grad_scores = (weights * (grad_weights - row_delta)).astype(jnp.bfloat16)
            query_grads = (
                query_grads
                + jnp.einsum(
                    "bhgqk,bkhd->bqhgd", grad_scores, key_part, preferred_element_type=jnp.float32
                )
                * factor
            )
            grad_keys = (
                jnp.einsum(
                    "bhgqk,bqhgd->kbhd", grad_scores, queries, preferred_element_type=jnp.float32
                )
                * factor
            )
            grad_values = jnp.einsum(
                "bhgqk,bqhgd->kbhd",
                weights.astype(jnp.bfloat16),
                grad_mixed,
                preferred_element_type=jnp.float32,
            )
            piece = jnp.concatenate(
                [
                    grad_keys.reshape(key_block, streams, kv_width),
                    grad_values.reshape(key_block, streams, kv_width),
                ],
                axis=-1,
            )
            key_terms_all = lax.dynamic_update_slice_in_dim(key_terms_all, piece, first_key, 0)
            return (query_grads, key_terms_all)

        return lax.cond(touches(first_key, key_block), back_compute, lambda state: state, running)

    grad_queries, key_terms_all = lax.fori_loop(
        0,
        blocks,
        back_block,
        (
            jnp.zeros((streams, length, KVH, group_size, HD), jnp.float32),
            jnp.zeros((stream_len, streams, 2 * kv_width), jnp.float32),
        ),
    )
    key_grads = summed_on_arrival(key_terms_all.astype(jnp.bfloat16), "seq", 0)
    key_grads = key_grads.transpose(1, 0, 2).reshape(tokens, 2 * kv_width)
    grad_q_lin = unrotate(grad_queries.reshape(tokens, HEADS, HD), cos_table, sin_table).reshape(
        tokens, q_width
    )
    grad_k_lin = unrotate(
        key_grads[:, :kv_width].reshape(tokens, KVH, HD), cos_table, sin_table
    ).reshape(tokens, kv_width)
    grad_projected = jnp.concatenate(
        [grad_q_lin, grad_k_lin, key_grads[:, kv_width:]], axis=1
    ).astype(jnp.bfloat16)
    grad_normed = transposed_product(grad_projected, w_qkv)
    scaled_attn = grad_normed * gain_attn
    grad_input = grad_middle + inv_attn * (
        scaled_attn - unit_attn * jnp.mean(scaled_attn * unit_attn, axis=-1, keepdims=True)
    )
    gain_attn_part = jnp.sum(grad_normed * unit_attn, axis=0)
    bias_part = jnp.sum(grad_projected.astype(jnp.float32), axis=0)

    def make_rows():

        def product(left, right):
            return lax.dot_general(
                left, right, (((0,), (0,)), ((), ())), preferred_element_type=jnp.float32
            )

        def row_terms(first_col, col_count):
            return jnp.concatenate(
                [
                    product(normed, grad_projected),
                    product(mixed_low, grad_branch),
                    product(normed_mlp, grad_gate_up),
                ],
                axis=1,
            )

        def down_terms(first_col, col_count):
            return product(active, seed_grad)

        return (row_terms, down_terms)

    row_share = model_width // lax.axis_size("seq")
    hidden_share = FF // lax.axis_size("seq")
    row_terms, down_terms = make_rows()
    row_part = lax.psum_scatter(
        row_terms(jnp.int32(0), row_share * lax.axis_size("seq")),
        "seq",
        scatter_dimension=0,
        tiled=True,
    )
    down_part = summed_on_arrival(
        down_terms(jnp.int32(0), hidden_share * lax.axis_size("seq")).astype(jnp.bfloat16), "seq", 0
    )
    row_part, down_part = (
        lax.psum(row_part.astype(jnp.bfloat16), "dp").astype(jnp.float32),
        lax.psum(down_part.astype(jnp.bfloat16), "dp").astype(jnp.float32),
    )
    bias_grad, gain_attn_grad, gain_mlp_grad = lax.psum(
        (bias_part, gain_attn_part, gain_mlp_part), ("seq", "dp")
    )
    joined_width = q_width + 2 * kv_width
    return (
        output.reshape(streams, length, model_width),
        grad_input.reshape(streams, length, model_width),
        row_part[:, :joined_width],
        bias_grad,
        gain_attn_grad,
        row_part[:, joined_width : joined_width + model_width],
        gain_mlp_grad,
        row_part[:, joined_width + model_width :],
        down_part,
    )


def solution(mesh):
    in_specs = (
        P("dp", "seq", None),
        P("dp", None),
        P(),
        P(),
        P(),
        P(),
        P(),
        P(),
        P(),
        P("dp", "seq", None),
    )
    out_specs = (
        P("dp", "seq", None),
        P("dp", "seq", None),
        P("seq", None),
        P(),
        P(),
        P("seq", None),
        P(),
        P("seq", None),
        P("seq", None),
    )
    return jax.shard_map(shards, mesh=mesh, in_specs=in_specs, out_specs=out_specs, check_vma=False)
```

profile of v0, /device:TPU:6, one launch (start us, length us, event | category | flops | bytes accessed | tf_op | source)
XLA Modules:
  0.0 1464.1 jit_solution(16891637317464104812)
XLA Ops:
  29.2 46.4 %all-gather.5.cloned.1.call-done = bf16[4,1536,128]{2,0,1:T(4,128)(2,1)} async-done(((bf16[4,96,128]{2,0,1:T(4,128)(2,1)}), bf16[4,1536,128]{2,0,1:T(4,128)(2,1)}) %all-gather.5.cloned.1.call-update) | async-done | bytes 1572880 | tf_op jit(solution)/shard_map/all_gather | solution.py:98
  79.5 15.1 %while.58 = (s32[]{:T(128)}, f32[4,2,7,96,1]{3,2,1,0,4:T(8,128)S(1)}, f32[4,2,7,96,1]{3,2,1,0,4:T(8,128)S(1)}, s32[96]{0:T(128)S(1)}, s32[4,1536]{1,0:T(4,128)S(...) while((s32[]{:T(128)}, ...), condition=%wide.region_11.12_spmd, body=%wide.region_5.11_spmd.sunk | while | flops 374795296 | bytes 24231176 | solution.py:146
  82.1 7.2 conditional.6
  94.6 40.9 %all-gather.3.cloned.1.call-done = bf16[4,1536,128]{2,1,0:T(8,128)(2,1)} async-done(((bf16[4,96,128]{2,1,0:T(8,128)(2,1)}), bf16[4,1536,128]{2,1,0:T(8,128)(2,1)}) %all-gather.3.cloned.1.call-update) | async-done | bytes 1572880 | tf_op jit(solution)/shard_map/all_gather | solution.py:99
  139.5 15.9 %while.59 = (s32[]{:T(128)}, f32[4,96,2,7,64]{1,4,3,2,0:T(8,128)}, s32[96]{0:T(128)S(1)}, s32[4,1536]{1,0:T(4,128)S(1)}, s32[4,96]{1,0:T(4,128)S(1)}, /*index=5*...) while((s32[]{:T(128)}, f32[4,96,2,7,64]{1,4,3,2,0:T(8,128)}, ...), condition=%wide.region_16.17_spmd, body=%wide.region_12.16_spmd.sunk | while | flops 716440064 | bytes 5492981 | solution.py:172
  142.1 8.1 conditional.7
  142.5 7.7 bitcast_add_fusion.1
  164.3 17.4 %fusion.57 = f32[384,9728]{1,0:T(8,128)} fusion(bf16[896,9728]{1,0:T(8,128)(2,1)} %param.29, f32[384,896]{1,0:T(8,128)S(1)} %get-tuple-element.1328, f32[896]{0:T(1024)S(1)} %convert_element_type.166, f32[384]{0:T(512)S(1)} %add_rsqrt_fusion), kind=kOutput, calls=%fused_computation.134 | convolution fusion | flops 6695141376 | bytes 33756160 | tf_op jit(solution)/shard_map/dot_general | solution.py:181
  181.7 14.5 multiply_convert_fusion.1
  196.2 16.0 %multiply_reduce_fusion = (f32[896]{0:T(1024)}, f32[384]{0:T(512)S(1)}, f32[384,896]{1,0:T(8,128)}) fusion(f32[384,896]{1,0:T(8,128)} %copy-done.8, f32[384]{0:T(512)S(1)} %add_rsqrt_fusion, f32[896]{0:T(1024)S(1)} %convert_element_type.166, bf16[896,9728]{1,0:T(8,128)(2,1)} %param.29, bf16[384,4864]{1,0:T(8,128)(2,1)} %get-tuple-element.1315, ...), kind=kOutput, calls=%fused_computation.84 | convolution fusion | flops 6711114240 | bytes 27666432 | tf_op jit(solution)/shard_map/dot_general | solution.py:60
  231.2 25.8 %while.60 = (s32[]{:T(128)}, f32[4,96,2,7,64]{1,4,3,2,0:T(8,128)}, bf16[1536,4,256]{0,2,1:T(8,128)(2,1)}, s32[96]{0:T(128)S(1)}, s32[4,1536]{1,0:T(4,128)S(1)}, ...) while((s32[]{:T(128)}, f32[4,96,2,7,64]{1,4,3,2,0:T(8,128)}, ...), condition=%wide.region_24.25_spmd, body=%wide.region_20.24_spmd.sunk | while | flops 1792885248 | bytes 74315176 | solution.py:262
  233.8 18.0 %conditional.8 = ((f32[4,96,2,7,64]{1,4,3,2,0:T(8,128)}, bf16[1536,4,256]{0,2,1:T(8,128)(2,1)})) conditional(s32[]{:T(128)} %convert_element_type.222, (f32[4,96,2,7,64]{1,4,3,2,0:T(8,128)}, bf16[1536,4,256]{0,2,1:T(8,128)(2,1)}) %tuple.195, (s32[]{:T(128)}, bf16[4,1536,2,64]{1,3,2,0:T(8,128)(2,1)}, s32[4,96]{1,0:T(4,128)S(1)}, ...), branch_computations={%region_22.22_spmd, %region_23.23_spmd} | conditional | flops 1792885248 | bytes 74314792 | solution.py:260
  239.8 5.0 fusion.26
  265.6 57.8 %all-to-all-start = ((bf16[16,96,4,256]{3,1,2,0:T(8,128)(2,1)}), bf16[16,96,4,256]{3,1,2,0:T(8,128)(2,1)}, u32[]{:S(2)}, u32[]{:S(2)}) async-start(bf16[16,96,4,256]{3,1,2,0:T(8,128)(2,1)} %copy.118), calls=%async_computation | async-start | bytes 6291456 | tf_op jit(solution)/shard_map/all_to_all | solution.py:21
  335.8 18.5 %fusion.47 = f32[896,9728]{1,0:T(8,128)} fusion(bf16[384,4864]{1,0:T(8,128)(2,1)} %get-tuple-element.1315, bf16[384,4864]{1,0:T(8,128)(2,1)} %get-tuple-element.1314, f32[384,896]{1,0:T(8,128)} %copy-done.8, f32[896]{0:T(1024)S(1)} %convert_element_type.166, f32[384]{0:T(512)S(1)} %add_rsqrt_fusion), kind=kOutput, calls=%fused_computation.76 | convolution fusion | flops 6710083584 | bytes 43717632 | tf_op jit(solution)/shard_map/dot_general | solution.py:293
  354.3 31.3 %all-to-all-done = bf16[16,96,4,256]{3,1,2,0:T(8,128)(2,1)} async-done(((bf16[16,96,4,256]{3,1,2,0:T(8,128)(2,1)}), bf16[16,96,4,256]{3,1,2,0:T(8,128)(2,1)}, u32[]{:S(2)}, u32[]{:S(2)}) %all-to-all-start) | async-done | bytes 3145760 | tf_op jit(solution)/shard_map/all_to_all | solution.py:21
  393.8 4.8 fusion.58
  398.6 29.1 %pad_maximum_fusion = f32[896,11776]{1,0:T(8,128)} fusion(f32[896,9728]{1,0:T(8,128)} %fusion.47, f32[896,896]{1,0:T(8,128)} %fusion.50, f32[896,1152]{1,0:T(8,128)} %fusion.58), kind=kLoop, calls=%fused_computation.67 | loop fusion | flops 21102592 | bytes 84410368 | tf_op jit(solution)/shard_map/concatenate | solution.py:298
  427.8 7.2 convolution_convert_fusion
  435.0 292.5 %all_to_all.10 = bf16[16,304,896]{2,1,0:T(8,128)(2,1)} all-to-all(bf16[16,304,896]{2,1,0:T(8,128)(2,1)S(1)} %bitcast.171), channel_id=1, replica_groups=mesh['seq'=16,'dp'=2] {'seq'}, dimensions={0} | all-to-all | bytes 17432576 | tf_op jit(solution)/shard_map/all_to_all | solution.py:21
  727.4 5.8 reduce_sum.141
  733.2 653.0 %reduce-scatter.2.cloned.1.call-done = f32[56,11776]{1,0:T(8,128)} async-done(((f32[896,11776]{1,0:T(8,128)}), f32[56,11776]{1,0:T(8,128)}) %reduce-scatter.2.cloned.1.call-update) | async-done | bytes 2637840 | tf_op jit(solution)/shard_map/reduce_scatter | solution.py:315
  1389.3 9.9 add_convert_fusion
  1402.4 44.2 %all-reduce = (f32[1152]{0:T(1024)}, f32[896]{0:T(1024)}, f32[896]{0:T(1024)}) all-reduce(f32[1152]{0:T(1024)S(1)} %convert_reduce_fusion.1, f32[896]{0:T(1024)} %get-tuple-element.1245, f32[896]{0:T(1024)} %get-tuple-element.1243), channel_id=1, replica_groups=mesh['seq'=16,'dp'=2] {'seq','dp'}, use_global_device_ids=true, to_apply=%region_30.31 | all-reduce | flops 2944 | bytes 23552 | tf_op jit(solution)/shard_map/psum | solution.py:328
  (192 shorter events, 135.5 us)
Async XLA Ops:
  7.2 6.3 copy-start
  7.2 68.4 %all-gather.5.cloned.1.call-start = ((), (), s32[]{:S(2)}) async-start(), calls=%async_computation.4 | async-start | bytes 1671168 | tf_op jit(solution)/shard_map/all_gather | solution.py:98
  10.4 4.2 copy-start.25
  11.1 3.5 copy-start.23
  11.2 3.4 copy-start.21
  16.0 5.4 copy-start.27
  16.3 6.9 copy-start.13
  16.3 6.9 copy-start.15
  17.3 118.2 %all-gather.3.cloned.1.call-start = ((), (), s32[]{:S(2)}) async-start(), calls=%async_computation.3 | async-start | bytes 1671168 | tf_op jit(solution)/shard_map/all_gather | solution.py:99
  164.2 17.5 %copy-start.8 = (f32[384,896]{1,0:T(8,128)}, f32[384,896]{1,0:T(8,128)S(1)}, u32[]{:S(2)}) copy-start(f32[384,896]{1,0:T(8,128)S(1)} %get-tuple-element.1328) | copy-start | bytes 4128772
  164.3 17.4 %copy-start.10 = (bf16[4,96,896]{2,1,0:T(8,128)(2,1)S(1)}, bf16[4,96,896]{2,1,0:T(8,128)(2,1)}, u32[]{:S(2)}) copy-start(bf16[4,96,896]{2,1,0:T(8,128)(2,1)} %broadcast_multiply_fusion) | copy-start | bytes 2064388
  212.2 3.6 copy-start.28
  223.3 3.4 copy-start.5
  265.6 120.0 %all-to-all-start = ((bf16[16,96,4,256]{3,1,2,0:T(8,128)(2,1)}), bf16[16,96,4,256]{3,1,2,0:T(8,128)(2,1)}, u32[]{:S(2)}, u32[]{:S(2)}) async-start(bf16[16,96,4,256]{3,1,2,0:T(8,128)(2,1)} %copy.118), calls=%async_computation | async-start | bytes 6291456 | tf_op jit(solution)/shard_map/all_to_all | solution.py:21
  323.3 1063.0 %reduce-scatter.2.cloned.1.call-start = ((), (), s32[]{:S(2)}) async-start(), calls=%async_computation.5 | async-start | bytes 44843008 | tf_op jit(solution)/shard_map/reduce_scatter | solution.py:315
  327.3 3.1 copy-start.14
  327.3 3.1 copy-start.16
  427.7 1022.6 %all-reduce.4.cloned.1.call-start = ((), (), s32[]{:S(2)}) async-start(), calls=%async_computation.6 | async-start | bytes 3727360 | tf_op jit(solution)/shard_map/psum | solution.py:325
  1389.2 9.9 copy-start.7
  1389.2 9.9 copy-start.18
  1389.3 10.2 copy-start.6
  1389.3 10.2 copy-start.24
  1389.3 10.1 copy-start.26
  1453.5 2.8 copy-start.20
  (10 other events, 18.1 us)
Sparse Core Ops, SparseCore 0:
  17.4 58.1 all-gather.4
  78.8 56.6 all-gather.2
  427.9 958.3 reduce-scatter.1
  1389.4 22.3 all-reduce.3
where the time goes:
time: 1470 us; the launch traced here: 1460 us
  waiting for transfers between devices  772 us (53%)
  blocking collectives  337 us (23%)
  matrix products  126 us (9%)
  other arithmetic  76.5 us (5%)
  local copies, waits for them, and re-layouts  68.9 us (5%)
  starting transfers between devices  57.9 us (4%)
    reduce_scatter x1, waiting for transfers between devices, shards(): lax.psum_scatter(row_terms(jnp.int32(0), row_share * lax.axis_size('seq')...  653 us
    all_to_all x1, blocking collectives, summed_on_arrival(): lax.all_to_all(cut_along(shard, dim, devices), axis, 0, 0, tiled=True)  292 us
    all_to_all x1, starting transfers between devices, summed_on_arrival(): lax.all_to_all(cut_along(shard, dim, devices), axis, 0, 0, tiled=True)  57.8 us
    all_gather x1, waiting for transfers between devices, shards(): lax.all_gather(key_low, 'seq', axis=1, tiled=True)  46.4 us
    psum x1, blocking collectives, shards(): lax.psum((bias_part, gain_attn_part, gain_mlp_part), ('seq', 'dp'))  44.2 us
    all_gather x1, waiting for transfers between devices, shards(): lax.all_gather(value_low, 'seq', axis=1, tiled=True)  40.9 us
    dot_general x4, matrix products, transposed_product(): lax.dot_general(left, right, (((1,), (1,)), ((), ())), preferred_element_...  35.4 us
    dot_general x4, matrix products, product(): lax.dot_general(left, right, (((0,), (0,)), ((), ())), preferred_element_...  33.2 us
  transfers between devices with their start and end apart: 5, of which 4 were waited for; matrix products, arithmetic and copies ran while one was open for 6% of the time, Pallas kernels for 0%

commit v1 on v0

--- a/solution.py
+++ b/solution.py
@@ -325,8 +325,9 @@
         lax.psum(row_part.astype(jnp.bfloat16), "dp").astype(jnp.float32),
         lax.psum(down_part.astype(jnp.bfloat16), "dp").astype(jnp.float32),
     )
-    bias_grad, gain_attn_grad, gain_mlp_grad = lax.psum(
-        (bias_part, gain_attn_part, gain_mlp_part), ("seq", "dp")
+    fix_widths = lambda patch: lax.psum(lax.psum(patch, "dp"), "seq")
+    bias_grad, gain_attn_grad, gain_mlp_grad = fix_widths(
+        (bias_part, gain_attn_part, gain_mlp_part)
     )
     joined_width = q_width + 2 * kv_width
     return (

time: 1470 us -> 1500 us (1.020)
  blocking collectives: 337 us -> 363 us
    psum x1 -> x2, blocking collectives: 44.2 us -> 71.8 us  [shards(): fix_widths = lambda patch: lax.psum(lax.psum(patch, 'dp'), 'seq')]
where the time goes in v1:
time: 1500 us; the launch traced here: 1490 us
  waiting for transfers between devices  772 us (51%)
  blocking collectives  363 us (24%)
  matrix products  126 us (8%)
  other arithmetic  74.7 us (5%)
  local copies, waits for them, and re-layouts  64.7 us (4%)
  starting transfers between devices  57.9 us (4%)
    reduce_scatter x1, waiting for transfers between devices, shards(): lax.psum_scatter(row_terms(jnp.int32(0), row_share * lax.axis_size('seq')...  653 us
    all_to_all x1, blocking collectives, summed_on_arrival(): lax.all_to_all(cut_along(shard, dim, devices), axis, 0, 0, tiled=True)  291 us
    psum x2, blocking collectives, shards(): fix_widths = lambda patch: lax.psum(lax.psum(patch, 'dp'), 'seq')  71.8 us
    all_to_all x1, starting transfers between devices, summed_on_arrival(): lax.all_to_all(cut_along(shard, dim, devices), axis, 0, 0, tiled=True)  57.8 us
    all_gather x1, waiting for transfers between devices, shards(): lax.all_gather(key_low, 'seq', axis=1, tiled=True)  46.8 us
    all_gather x1, waiting for transfers between devices, shards(): lax.all_gather(value_low, 'seq', axis=1, tiled=True)  40.9 us
    dot_general x4, matrix products, transposed_product(): lax.dot_general(left, right, (((1,), (1,)), ((), ())), preferred_element_...  34.8 us
    dot_general x4, matrix products, product(): lax.dot_general(left, right, (((0,), (0,)), ((), ())), preferred_element_...  33.7 us
  transfers between devices with their start and end apart: 5, of which 4 were waited for; matrix products, arithmetic and copies ran while one was open for 6% of the time, Pallas kernels for 0%

profile of v1, /device:TPU:6, one launch (start us, length us, event | category | flops | bytes accessed | tf_op | source)
XLA Modules:
  0.0 1485.1 jit_solution(12301720233843938556)
XLA Ops:
  28.8 46.8 %all-gather.5.cloned.1.call-done = bf16[4,1536,128]{2,0,1:T(4,128)(2,1)} async-done(((bf16[4,96,128]{2,0,1:T(4,128)(2,1)}), bf16[4,1536,128]{2,0,1:T(4,128)(2,1)}) %all-gather.5.cloned.1.call-update) | async-done | bytes 1572880 | tf_op jit(solution)/shard_map/all_gather | solution.py:98
  79.5 15.1 %while.58 = (s32[]{:T(128)}, f32[4,2,7,96,1]{3,2,1,0,4:T(8,128)S(1)}, f32[4,2,7,96,1]{3,2,1,0,4:T(8,128)S(1)}, s32[96]{0:T(128)S(1)}, s32[4,1536]{1,0:T(4,128)S(...) while((s32[]{:T(128)}, ...), condition=%wide.region_11.12_spmd, body=%wide.region_5.11_spmd.sunk | while | flops 374795296 | bytes 24231176 | solution.py:146
  82.1 7.1 conditional.6
  94.6 40.9 %all-gather.3.cloned.1.call-done = bf16[4,1536,128]{2,1,0:T(8,128)(2,1)} async-done(((bf16[4,96,128]{2,1,0:T(8,128)(2,1)}), bf16[4,1536,128]{2,1,0:T(8,128)(2,1)}) %all-gather.3.cloned.1.call-update) | async-done | bytes 1572880 | tf_op jit(solution)/shard_map/all_gather | solution.py:99
  139.5 15.9 %while.59 = (s32[]{:T(128)}, f32[4,96,2,7,64]{1,4,3,2,0:T(8,128)}, s32[96]{0:T(128)S(1)}, s32[4,1536]{1,0:T(4,128)S(1)}, s32[4,96]{1,0:T(4,128)S(1)}, /*index=5*...) while((s32[]{:T(128)}, f32[4,96,2,7,64]{1,4,3,2,0:T(8,128)}, ...), condition=%wide.region_16.17_spmd, body=%wide.region_12.16_spmd.sunk | while | flops 716440064 | bytes 5492981 | solution.py:172
  142.1 8.1 conditional.7
  142.4 7.7 bitcast_add_fusion.1
  164.2 17.4 %fusion.57 = f32[384,9728]{1,0:T(8,128)} fusion(bf16[896,9728]{1,0:T(8,128)(2,1)} %param.29, f32[384,896]{1,0:T(8,128)S(1)} %get-tuple-element.1331, f32[896]{0:T(1024)S(1)} %convert_element_type.166, f32[384]{0:T(512)S(1)} %add_rsqrt_fusion), kind=kOutput, calls=%fused_computation.134 | convolution fusion | flops 6695141376 | bytes 33756160 | tf_op jit(solution)/shard_map/dot_general | solution.py:181
  181.7 14.5 multiply_convert_fusion.1
  196.2 16.0 %multiply_reduce_fusion = (f32[896]{0:T(1024)}, f32[384]{0:T(512)S(1)}, f32[384,896]{1,0:T(8,128)}) fusion(f32[384,896]{1,0:T(8,128)} %copy-done.9, f32[384]{0:T(512)S(1)} %add_rsqrt_fusion, f32[896]{0:T(1024)S(1)} %convert_element_type.166, bf16[896,9728]{1,0:T(8,128)(2,1)} %param.29, bf16[384,4864]{1,0:T(8,128)(2,1)} %get-tuple-element.1318, ...), kind=kOutput, calls=%fused_computation.84 | convolution fusion | flops 6711114240 | bytes 27666432 | tf_op jit(solution)/shard_map/dot_general | solution.py:60
  231.1 25.8 %while.60 = (s32[]{:T(128)}, f32[4,96,2,7,64]{1,4,3,2,0:T(8,128)}, bf16[1536,4,256]{0,2,1:T(8,128)(2,1)}, s32[96]{0:T(128)S(1)}, s32[4,1536]{1,0:T(4,128)S(1)}, ...) while((s32[]{:T(128)}, f32[4,96,2,7,64]{1,4,3,2,0:T(8,128)}, ...), condition=%wide.region_24.25_spmd, body=%wide.region_20.24_spmd.sunk | while | flops 1792885248 | bytes 74315176 | solution.py:262
  233.7 18.0 %conditional.8 = ((f32[4,96,2,7,64]{1,4,3,2,0:T(8,128)}, bf16[1536,4,256]{0,2,1:T(8,128)(2,1)})) conditional(s32[]{:T(128)} %convert_element_type.222, (f32[4,96,2,7,64]{1,4,3,2,0:T(8,128)}, bf16[1536,4,256]{0,2,1:T(8,128)(2,1)}) %tuple.195, (s32[]{:T(128)}, bf16[4,1536,2,64]{1,3,2,0:T(8,128)(2,1)}, s32[4,96]{1,0:T(4,128)S(1)}, ...), branch_computations={%region_22.22_spmd, %region_23.23_spmd} | conditional | flops 1792885248 | bytes 74314792 | solution.py:260
  239.7 5.0 fusion.26
  256.9 4.7 copy.117
  265.5 57.8 %all-to-all-start = ((bf16[16,96,4,256]{3,1,2,0:T(8,128)(2,1)}), bf16[16,96,4,256]{3,1,2,0:T(8,128)(2,1)}, u32[]{:S(2)}, u32[]{:S(2)}) async-start(bf16[16,96,4,256]{3,1,2,0:T(8,128)(2,1)} %copy.118), calls=%async_computation | async-start | bytes 6291456 | tf_op jit(solution)/shard_map/all_to_all | solution.py:21
  335.0 18.5 %fusion.47 = f32[896,9728]{1,0:T(8,128)} fusion(bf16[384,4864]{1,0:T(8,128)(2,1)} %get-tuple-element.1318, bf16[384,4864]{1,0:T(8,128)(2,1)} %get-tuple-element.1317, f32[384,896]{1,0:T(8,128)} %copy-done.9, f32[896]{0:T(1024)S(1)} %convert_element_type.166, f32[384]{0:T(512)S(1)} %add_rsqrt_fusion), kind=kOutput, calls=%fused_computation.76 | convolution fusion | flops 6710083584 | bytes 43717632 | tf_op jit(solution)/shard_map/dot_general | solution.py:293
  353.5 31.9 %all-to-all-done = bf16[16,96,4,256]{3,1,2,0:T(8,128)(2,1)} async-done(((bf16[16,96,4,256]{3,1,2,0:T(8,128)(2,1)}), bf16[16,96,4,256]{3,1,2,0:T(8,128)(2,1)}, u32[]{:S(2)}, u32[]{:S(2)}) %all-to-all-start) | async-done | bytes 3145760 | tf_op jit(solution)/shard_map/all_to_all | solution.py:21
  393.0 29.1 %pad_maximum_fusion = f32[896,11776]{1,0:T(8,128)} fusion(f32[896,9728]{1,0:T(8,128)} %fusion.47, f32[896,896]{1,0:T(8,128)} %fusion.50, f32[896,1152]{1,0:T(8,128)} %fusion.58), kind=kLoop, calls=%fused_computation.67 | loop fusion | flops 21102592 | bytes 84410368 | tf_op jit(solution)/shard_map/concatenate | solution.py:298
  423.1 7.9 convolution_convert_fusion
  431.0 291.0 %all_to_all.10 = bf16[16,304,896]{2,1,0:T(8,128)(2,1)} all-to-all(bf16[16,304,896]{2,1,0:T(8,128)(2,1)S(1)} %bitcast.171), channel_id=1, replica_groups=mesh['seq'=16,'dp'=2] {'seq'}, dimensions={0} | all-to-all | bytes 17432576 | tf_op jit(solution)/shard_map/all_to_all | solution.py:21
  722.0 5.8 reduce_sum.141
  727.8 652.8 %reduce-scatter.2.cloned.1.call-done = f32[56,11776]{1,0:T(8,128)} async-done(((f32[896,11776]{1,0:T(8,128)}), f32[56,11776]{1,0:T(8,128)}) %reduce-scatter.2.cloned.1.call-update) | async-done | bytes 2637840 | tf_op jit(solution)/shard_map/reduce_scatter | solution.py:315
  1383.6 9.9 add_convert_fusion
  1399.5 68.5 %all-reduce = (f32[1152]{0:T(1024)}, f32[896]{0:T(1024)}, f32[896]{0:T(1024)}) all-reduce(f32[1152]{0:T(1024)S(1)} %get-tuple-element.1310, f32[896]{0:T(1024)S(1)} %get-tuple-element.1311, f32[896]{0:T(1024)S(1)} %get-tuple-element.1312), channel_id=1, replica_groups=mesh['seq'=16,'dp'=2] {'seq'}, use_global_device_ids=true, to_apply=%region_31.32 | all-reduce | flops 2944 | bytes 23552 | tf_op jit(solution)/shard_map/psum | solution.py:328
  (193 shorter events, 132.2 us)
Async XLA Ops:
  7.2 6.3 copy-start
  7.2 68.4 %all-gather.5.cloned.1.call-start = ((), (), s32[]{:S(2)}) async-start(), calls=%async_computation.4 | async-start | bytes 1671168 | tf_op jit(solution)/shard_map/all_gather | solution.py:98
  10.4 4.2 copy-start.24
  11.1 3.5 copy-start.22
  16.0 5.4 copy-start.27
  16.3 8.0 copy-start.15
  16.3 8.0 copy-start.17
  17.3 118.2 %all-gather.3.cloned.1.call-start = ((), (), s32[]{:S(2)}) async-start(), calls=%async_computation.3 | async-start | bytes 1671168 | tf_op jit(solution)/shard_map/all_gather | solution.py:99
  164.2 17.5 %copy-start.9 = (f32[384,896]{1,0:T(8,128)}, f32[384,896]{1,0:T(8,128)S(1)}, u32[]{:S(2)}) copy-start(f32[384,896]{1,0:T(8,128)S(1)} %get-tuple-element.1331) | copy-start | bytes 4128772
  164.2 17.4 %copy-start.11 = (bf16[4,96,896]{2,1,0:T(8,128)(2,1)S(1)}, bf16[4,96,896]{2,1,0:T(8,128)(2,1)}, u32[]{:S(2)}) copy-start(bf16[4,96,896]{2,1,0:T(8,128)(2,1)} %broadcast_multiply_fusion) | copy-start | bytes 2064388
  212.2 3.5 copy-start.28
  223.2 3.4 copy-start.5
  234.1 2.8 copy-start.19
  265.5 120.0 %all-to-all-start = ((bf16[16,96,4,256]{3,1,2,0:T(8,128)(2,1)}), bf16[16,96,4,256]{3,1,2,0:T(8,128)(2,1)}, u32[]{:S(2)}, u32[]{:S(2)}) async-start(bf16[16,96,4,256]{3,1,2,0:T(8,128)(2,1)} %copy.118), calls=%async_computation | async-start | bytes 6291456 | tf_op jit(solution)/shard_map/all_to_all | solution.py:21
  323.2 1057.4 %reduce-scatter.2.cloned.1.call-start = ((), (), s32[]{:S(2)}) async-start(), calls=%async_computation.5 | async-start | bytes 44843008 | tf_op jit(solution)/shard_map/reduce_scatter | solution.py:315
  327.2 3.1 copy-start.16
  327.2 3.1 copy-start.18
  332.3 56.1 %copy-start.7 = (bf16[384,14,64]{0,2,1:T(8,128)(2,1)}, bf16[384,14,64]{0,2,1:T(8,128)(2,1)S(1)}, u32[]{:S(2)}) copy-start(bf16[384,14,64]{0,2,1:T(8,128)(2,1)S(1)} %pad_maximum_fusion.6) | copy-start | bytes 2064388
  422.1 1049.2 %all-reduce.5.cloned.1.call-start = ((), (), s32[]{:S(2)}) async-start(), calls=%async_computation.6 | async-start | bytes 3727360 | tf_op jit(solution)/shard_map/psum | solution.py:325
  1383.6 9.9 copy-start.8
  1383.6 10.1 copy-start.6
  1383.6 10.1 copy-start.23
  1383.6 10.1 copy-start.25
  1474.5 2.8 copy-start.21
  (10 other events, 14.8 us)
Sparse Core Ops, SparseCore 0:
  17.4 58.0 all-gather.4
  78.8 56.6 all-gather.2
  422.2 958.3 reduce-scatter.1
  1383.7 22.2 all-reduce.4
